TPU v7x, 32 devices: a whole 2x2x4 slice. The times are simulated.
32 devices in a mesh: row: 8 (over z, x), col: 4 (over y, core).
Axes of the slice: x: 2, y: 2, z: 4, core: 2. Of those that a mesh axis runs over, the one named last changes fastest.
Arguments:
- sources_in: bfloat16 [32768, 2, 512], P(('row', 'col')), may hold values from -6 to 6
- right_bases: bfloat16 [64, 8, 2, 96, 512], P(('row', 'col')), may hold values from -0.1875 to 0.1875
- left_bases: bfloat16 [8, 8, 8, 2, 96, 512], P('row', None, 'col'), may hold values from -0.046875 to 0.046875
- tile_ranks: int32 [8, 64], P(None, ('row', 'col')), may hold values from 16 to 96
Outputs:
- redatumed: bfloat16 [4096, 2, 512], P(('row', 'col'))
Inputs may be any that keep to these rules, and one draw needn't show every extreme that they name: `tile_ranks`: each tile's rank; rows of its bases at or beyond it do not count.
All inputs are finite; a program needn't handle non-finite values.
Results may differ from a plain program's by a relative error of at most 0.0049.
Values may be sent and summed in bfloat16 or wider, within the bound.
A program may use at most 256 MiB of HBM per device.

v0:
```python
import jax
import jax.numpy as jnp
from jax import lax
from jax.sharding import PartitionSpec as P


def complex_rows(prod):
    real = prod[:, 0, 0] - prod[:, 1, 1]
    imag = prod[:, 0, 1] + prod[:, 1, 0]
    return jnp.stack([real, imag], 1)


def body(sources_in, right_bases, left_bases, tile_ranks):
    cols, tile_rows, _, rank_pad, width = right_bases.shape
    samples = sources_in.shape[2]
    blocks = sources_in.reshape(cols, width, 2, samples)
    prod = jnp.einsum("cmprb,cbqs->cmpqrs", right_bases, blocks, preferred_element_type=jnp.float32)
    real = prod[:, :, 0, 0] - prod[:, :, 1, 1]
    imag = prod[:, :, 0, 1] + prod[:, :, 1, 0]
    levels = lax.broadcasted_iota(jnp.int32, (cols, tile_rows, rank_pad), 2)
    keep = (levels < tile_ranks.T[:, :, None]).astype(jnp.float32)
    coeffs = (jnp.stack([real, imag], 2) * keep[:, :, None, :, None]).astype(jnp.bfloat16)
    left_flat = left_bases.reshape(-1, 2, rank_pad, width)
    picked = lax.all_to_all(coeffs, "row", split_axis=1, concat_axis=0, tiled=True)[:, 0]
    terms = jnp.einsum("jpkb,jqks->bpqs", left_flat, picked, preferred_element_type=jnp.float32)
    partial_value = complex_rows(terms)
    return lax.psum_scatter(partial_value, "col", scatter_dimension=0, tiled=True).astype(
        jnp.bfloat16
    )


def solution(mesh):
    in_specs = (
        P(("row", "col"), None, None),
        P(("row", "col"), None, None, None, None),
        P("row", None, "col", None, None, None),
        P(None, ("row", "col")),
    )
    out_specs = P(("row", "col"), None, None)
    return jax.shard_map(body, mesh=mesh, in_specs=in_specs, out_specs=out_specs, check_vma=False)
```

profile of v0, /device:TPU:0, one launch (start us, length us, event | category | flops | bytes accessed | tf_op | source)
XLA Modules:
  0.0 140.6 jit_solution(18144170342708530463)
XLA Ops:
  6.5 0.0 copy-start
  6.5 0.0 reduce-scatter.2.cloned.1.call-start
  6.5 1.9 %copy-done = bf16[2,8,2,96,512]{4,3,2,1,0:T(8,128)(2,1)S(1)} copy-done((bf16[2,8,2,96,512]{4,3,2,1,0:T(8,128)(2,1)S(1)}, bf16[2,8,2,96,512]{4,3,2,1,0:T(8,128)(2,1)}, u32[]{:S(2)}) %copy-start) | copy-done | bytes 3145752
  8.4 5.0 %convolution_bitcast_fusion = f32[2,8,2,2,96,512]{5,4,2,1,3,0:T(8,128)S(1)} fusion(bf16[2,8,2,96,512]{4,3,2,1,0:T(8,128)(2,1)S(1)} %copy-done, bf16[2,512,2,512,1,1]{3,2,1,0,5,4:T(2,128)(2,1)} %bitcast.60), kind=kOutput, calls=%fused_computation.2 | convolution fusion | flops 3221225472 | bytes 17825792 | tf_op jit(solution)/shard_map/cmprb,cbqs->cmpqrs/dot_general | solution.py:17
  13.4 0.9 fusion.1
  14.3 0.0 copy-start.1
  14.3 0.9 fusion.3
  15.2 0.0 copy-done.1
  15.2 0.1 fusion.18
  15.3 0.5 fusion
  15.8 0.3 copy.24
  16.1 77.8 %all_to_all.15 = bf16[2,8,2,96,512]{4,3,0,2,1:T(8,128)(2,1)S(1)} all-to-all(bf16[2,8,2,96,512]{4,3,0,2,1:T(8,128)(2,1)S(1)} %copy.24), channel_id=1, replica_groups=mesh['row'=8,'col'=4] {'row'}, dimensions={1} | all-to-all | bytes 6291456 | tf_op jit(solution)/shard_map/all_to_all | solution.py:24
  93.9 0.0 copy-start.2
  93.9 0.3 copy.25
  94.2 1.6 %copy-done.2 = bf16[1,8,2,2,96,512]{5,4,3,2,1,0:T(8,128)(2,1)S(1)} copy-done((bf16[1,8,2,2,96,512]{5,4,3,2,1,0:T(8,128)(2,1)S(1)}, bf16[1,8,2,2,96,512]{5,4,3,2,1,0:T(8,128)(2,1)}, u32[]{:S(2)}) %copy-start.2) | copy-done | bytes 3145752
  95.8 3.5 %fusion.9 = f32[512,2,2,512]{0,3,1,2:T(8,128)S(1)} fusion(bf16[16,2,96,512]{3,2,1,0:T(8,128)(2,1)S(1)} %bitcast.59, bf16[16,2,96,512,1]{3,2,1,0,4:T(8,128)(2,1)S(1)} %bitcast.57), kind=kOutput, calls=%fused_computation.14 | convolution fusion | flops 3221225472 | bytes 10485760 | tf_op jit(solution)/shard_map/jpkb,jqks->bpqs/dot_general | solution.py:25
  99.2 0.2 fusion.15
  99.4 0.2 fusion.17
  99.7 1.5 %pad_maximum_fusion = f32[512,2,512]{0,2,1:T(8,128)} fusion(f32[512,1,512]{0,2,1:T(8,128)S(1)} %fusion.15, f32[512,1,512]{0,2,1:T(8,128)S(1)} %fusion.17), kind=kLoop, calls=%fused_computation.15 | loop fusion | flops 524288 | bytes 4194304 | tf_op jit(solution)/shard_map/stack | solution.py:10
  101.2 0.0 reduce-scatter.2.cloned.1.call-update
  101.2 30.6 %reduce-scatter.2.cloned.1.call-done = f32[128,2,512]{0,2,1:T(8,128)} async-done(((f32[512,2,512]{0,2,1:T(8,128)}), f32[128,2,512]{0,2,1:T(8,128)}) %reduce-scatter.2.cloned.1.call-update) | async-done | bytes 524304 | tf_op jit(solution)/shard_map/reduce_scatter | solution.py:27
  131.8 1.1 convert_element_type.15
  132.9 0.9 copy.30
Async XLA Ops:
  6.5 1.9 %copy-start = (bf16[2,8,2,96,512]{4,3,2,1,0:T(8,128)(2,1)S(1)}, bf16[2,8,2,96,512]{4,3,2,1,0:T(8,128)(2,1)}, u32[]{:S(2)}) copy-start(bf16[2,8,2,96,512]{4,3,2,1,0:T(8,128)(2,1)} %param.5) | copy-start | bytes 9437188
  6.5 125.2 %reduce-scatter.2.cloned.1.call-start = ((), (), s32[]{:S(2)}) async-start(), calls=%async_computation.2 | async-start | bytes 2621440 | tf_op jit(solution)/shard_map/reduce_scatter | solution.py:27
  14.3 0.9 copy-start.1
  93.9 1.9 %copy-start.2 = (bf16[1,8,2,2,96,512]{5,4,3,2,1,0:T(8,128)(2,1)S(1)}, bf16[1,8,2,2,96,512]{5,4,3,2,1,0:T(8,128)(2,1)}, u32[]{:S(2)}) copy-start(bf16[1,8,2,2,96,512]{5,4,3,2,1,0:T(8,128)(2,1)} %param.6) | copy-start | bytes 9437188
Sparse Core Ops, SparseCore 0:
  101.3 30.4 reduce-scatter.1
where the time goes:
time: 141 us
  blocking collectives  77.8 us (55%)
  waiting for transfers between devices  30.6 us (22%)
  between operations  13.5 us (10%)
  matrix products  8.46 us (6%)
  other arithmetic  5.29 us (4%)
  local copies, waits for them, and re-layouts  4.98 us (4%)
    all_to_all x1, blocking collectives, body(): lax.all_to_all(coeffs, 'row', split_axis=1, concat_axis=0, tiled=True)[:, 0]  77.8 us
    reduce_scatter x1, waiting for transfers between devices, body(): lax.psum_scatter(partial_value, 'col', scatter_dimension=0, tiled=True)  30.6 us
    dot_general x1, matrix products, body(): jnp.einsum('cmprb,cbqs->cmpqrs', right_bases, blocks, preferred_element_t...  5 us
    dot_general x1, matrix products, body(): jnp.einsum('jpkb,jqks->bpqs', left_flat, picked, preferred_element_type=j...  3.46 us
    unnamed x6, local copies, waits for them, and re-layouts  3.46 us
  transfers between devices with their start and end apart: 1, of which 1 were waited for; matrix products, arithmetic and copies ran while one was open for 0% of the time, Pallas kernels for 0%

commit v1 on v0

v1 whole, which is shorter than its diff:
```python
import functools

import jax
import jax.numpy as jnp
from jax import lax
from jax.experimental import pallas as pl
from jax.experimental.pallas import tpu as pltpu
from jax.sharding import PartitionSpec as P

MESH = pl.DeviceIdType.MESH
CHUNK = 128


def apply_kernel(
    n_row, n_col, coef, left, out, held, basis, total, outgoing, partial,
    send_sem, recv_sem, psend_sem, precv_sem,
):
    row, col = lax.axis_index("row"), lax.axis_index("col")
    half = n_row // 2
    side = row // half
    place = row % half
    depth, samples = coef.shape[1], coef.shape[2]
    tiles, _, rank_pad, width = left.shape
    cols = tiles // n_row
    chunks = samples // CHUNK
    share = width // n_col

    def to_row(k):
        far = k < half
        there = jnp.where(far, 1 - side, side)
        return there * half + (place + k) % half

    def from_row(k):
        far = k < half
        there = jnp.where(far, 1 - side, side)
        return there * half + (place + 2 * half - k) % half

    steps = [k for k in range(n_row) if k != half]

    barrier = pltpu.get_barrier_semaphore()
    for k in range(1, n_row):
        pl.semaphore_signal(barrier, inc=1, device_id={"row": (row + k) % n_row}, device_id_type=MESH)
    for k in range(1, n_col):
        pl.semaphore_signal(barrier, inc=1, device_id={"col": (col + k) % n_col}, device_id_type=MESH)
    pl.semaphore_wait(barrier, n_row + n_col - 2)

    def coef_copy(k, dest, slot, ch):
        lanes = pl.ds(ch * CHUNK, CHUNK)
        return pltpu.make_async_remote_copy(
            src_ref=coef.at[dest, :, lanes],
            dst_ref=held.at[slot, :, lanes],
            send_sem=send_sem.at[k, ch],
            recv_sem=recv_sem.at[k, ch],
            device_id={"row": dest},
            device_id_type=MESH,
        )

    for ch in range(chunks):
        for k in steps:
            coef_copy(k, to_row(k), row, ch).start()

    def prepare(a, carry):
        plain, swapped = [], []
        for c in range(cols):
            real, imag = left[a * cols + c, 0], left[a * cols + c, 1]
            plain += [real, -imag]
            swapped += [imag, real]
        basis[a, 0:width, :] = jnp.concatenate(plain, 0).T
        basis[a, width : 2 * width, :] = jnp.concatenate(swapped, 0).T
        return carry

    lax.fori_loop(0, n_row, prepare, 0)

    def partial_copy(k, ch):
        dest = (col + k) % n_col
        return pltpu.make_async_remote_copy(
            src_ref=outgoing.at[ch, :, pl.ds(pl.multiple_of(dest * share, share), share)],
            dst_ref=partial.at[ch, k - 1],
            send_sem=psend_sem.at[k, ch],
            recv_sem=precv_sem.at[k, ch],
            device_id={"col": dest},
            device_id_type=MESH,
        )

    def finish(ch):
        lanes = pl.ds(ch * CHUNK, CHUNK)
        mine = outgoing[ch, :, pl.ds(pl.multiple_of(col * share, share), share), :]
        for k in range(1, n_col):
            partial_copy(k, ch).wait_recv()
            mine = mine + partial[ch, k - 1]
        out[:, :, lanes] = mine.astype(out.dtype)

    for ch in range(chunks):
        lanes = pl.ds(ch * CHUNK, CHUNK)
        total[...] = jnp.dot(basis[row], coef[row, :, lanes], preferred_element_type=jnp.float32)

        def take(k, carry):
            source = from_row(k)
            coef_copy(k, to_row(k), source, ch).wait_recv()
            total[...] += jnp.dot(basis[source], held[source, :, lanes], preferred_element_type=jnp.float32)
            return carry

        lax.fori_loop(half + 1, n_row, take, 0)
        lax.fori_loop(0, half, take, 0)
        outgoing[ch] = total[...].reshape(2, width, CHUNK)
        for k in range(1, n_col):
            partial_copy(k, ch).start()
        if ch > 0:
            finish(ch - 1)
    finish(chunks - 1)
    for ch in range(chunks):
        for k in steps:
            coef_copy(k, to_row(k), row, ch).wait_send()
        for k in range(1, n_col):
            partial_copy(k, ch).wait_send()


def body(n_row, n_col, sources_in, right_bases, left_bases, tile_ranks):
    cols, tile_rows, _, rank_pad, width = right_bases.shape
    samples = sources_in.shape[2]
    blocks = sources_in.reshape(cols, width, 2, samples)
    prod = jnp.einsum("cmprb,cbqs->cmpqrs", right_bases, blocks, preferred_element_type=jnp.float32)
    real = prod[:, :, 0, 0] - prod[:, :, 1, 1]
    imag = prod[:, :, 0, 1] + prod[:, :, 1, 0]
    levels = lax.broadcasted_iota(jnp.int32, (cols, tile_rows, rank_pad), 2)
    keep = (levels < tile_ranks.T[:, :, None]).astype(jnp.float32)
    coeffs = (jnp.stack([real, imag], 2) * keep[:, :, None, :, None]).astype(jnp.bfloat16)
    depth = cols * 2 * rank_pad
    coeffs = coeffs.transpose(1, 0, 2, 3, 4).reshape(tile_rows, depth, samples)
    left = left_bases.reshape(-1, 2, rank_pad, width)
    chunks = samples // CHUNK
    share = width // n_col
    vmem = pl.BlockSpec(memory_space=pltpu.VMEM)
    out = pl.pallas_call(
        functools.partial(apply_kernel, n_row, n_col),
        out_shape=jax.ShapeDtypeStruct((2, share, samples), jnp.bfloat16),
        in_specs=[vmem, vmem],
        out_specs=vmem,
        scratch_shapes=[
            pltpu.VMEM((n_row, depth, samples), jnp.bfloat16),
            pltpu.VMEM((n_row, 2 * width, depth), jnp.bfloat16),
            pltpu.VMEM((2 * width, CHUNK), jnp.float32),
            pltpu.VMEM((chunks, 2, width, CHUNK), jnp.float32),
            pltpu.VMEM((chunks, n_col - 1, 2, share, CHUNK), jnp.float32),
            pltpu.SemaphoreType.DMA((n_row, chunks)),
            pltpu.SemaphoreType.DMA((n_row, chunks)),
            pltpu.SemaphoreType.DMA((n_col, chunks)),
            pltpu.SemaphoreType.DMA((n_col, chunks)),
        ],
        compiler_params=pltpu.CompilerParams(
            collective_id=0, has_side_effects=True, vmem_limit_bytes=56 * 2**20
        ),
    )(coeffs, left)
    return out.transpose(1, 0, 2)


def solution(mesh):
    in_specs = (
        P(("row", "col"), None, None),
        P(("row", "col"), None, None, None, None),
        P("row", None, "col", None, None, None),
        P(None, ("row", "col")),
    )
    return jax.shard_map(
        functools.partial(body, mesh.shape["row"], mesh.shape["col"]),
        mesh=mesh,
        in_specs=in_specs,
        out_specs=P(("row", "col"), None, None),
        check_vma=False,
    )
```

time: 141 us -> 99.9 us (0.71)
  Pallas kernels: 0 us -> 86.5 us
  blocking collectives: 77.8 us -> 0 us
  waiting for transfers between devices: 30.6 us -> 0 us
  between operations: 13.5 us -> 0.06 us
  matrix products: 8.46 us -> 5 us
  other arithmetic: 5.29 us -> 2.29 us
    pallas_call x0 -> x1, Pallas kernels: none -> 86.5 us  [body(): pl.pallas_call(functools.partial(apply_kernel, n_row, n_col), out_shape=j...]
    all_to_all x1 -> x0, blocking collectives: 77.8 us -> none  [body(): lax.all_to_all(coeffs, 'row', split_axis=1, concat_axis=0, tiled=True)[:, 0]]
    reduce_scatter x1 -> x0, waiting for transfers between devices: 30.6 us -> none  [body(): lax.psum_scatter(partial_value, 'col', scatter_dimension=0, tiled=True)]
    transpose x0 -> x2, local copies, waits for them, and re-layouts: none -> 3.91 us  [the longest x1 1.99 us: body(): coeffs = coeffs.transpose(1, 0, 2, 3, 4).reshape(tile_rows, depth, samples)]
    dot_general x1 -> x0, matrix products: 3.46 us -> none  [body(): jnp.einsum('jpkb,jqks->bpqs', left_flat, picked, preferred_element_type=j...]
    convert_element_type x2 -> x0, other arithmetic: 1.58 us -> none  [the longest x1 1.08 us: body(): lax.psum_scatter(partial_value, 'col', scatter_dimension=0, tiled=True)]
    unnamed x6 -> x4, local copies, waits for them, and re-layouts: 3.46 us -> 1.9 us
    another operation x1 -> x0, other arithmetic: 1.5 us -> none  [complex_rows(): return jnp.stack([real, imag], 1)]
  transfers between devices with their start and end apart: 1 -> 0, of which waited for: 1 -> 0; matrix products, arithmetic and copies ran while one was open for 0% -> 0% of each run, Pallas kernels for 0% -> 0%
where the time goes in v1:
time: 99.9 us; the launch traced here: 99.7 us
  Pallas kernels  86.5 us (87%)
  local copies, waits for them, and re-layouts  5.81 us (6%)
  matrix products  5 us (5%)
  other arithmetic  2.29 us (2%)
    pallas_call x1, Pallas kernels, body(): pl.pallas_call(functools.partial(apply_kernel, n_row, n_col), out_shape=j...  86.5 us
    dot_general x1, matrix products, body(): jnp.einsum('cmprb,cbqs->cmpqrs', right_bases, blocks, preferred_element_t...  5 us

profile of v1, /device:TPU:0, one launch (start us, length us, event | category | flops | bytes accessed | tf_op | source)
XLA Modules:
  0.0 99.7 jit_solution(4038968661292908991)
XLA Ops:
  0.0 0.0 copy-start
  0.0 1.9 %copy-done = bf16[2,8,2,96,512]{4,3,2,1,0:T(8,128)(2,1)S(1)} copy-done((bf16[2,8,2,96,512]{4,3,2,1,0:T(8,128)(2,1)S(1)}, bf16[2,8,2,96,512]{4,3,2,1,0:T(8,128)(2,1)}, u32[]{:S(2)}) %copy-start) | copy-done | bytes 3145752
  1.9 5.0 %convolution_bitcast_fusion = f32[2,8,2,2,96,512]{5,4,2,1,3,0:T(8,128)S(1)} fusion(bf16[2,8,2,96,512]{4,3,2,1,0:T(8,128)(2,1)S(1)} %copy-done, bf16[2,512,2,512,1,1]{3,2,1,0,5,4:T(2,128)(2,1)} %bitcast.34), kind=kOutput, calls=%fused_computation.2 | convolution fusion | flops 3221225472 | bytes 17825792 | tf_op jit(solution)/shard_map/cmprb,cbqs->cmpqrs/dot_general | solution.py:122
  6.9 0.9 fusion.2
  7.8 0.0 copy-start.1
  7.8 0.9 fusion.4
  8.6 0.0 copy-done.1
  8.7 0.1 fusion.7
  8.7 0.5 fusion.1
  9.2 2.0 %copy.8 = bf16[8,2,2,96,512]{4,3,2,1,0:T(8,128)(2,1)} copy(bf16[8,2,2,96,512]{4,3,0,1,2:T(8,128)(2,1)S(1)} %fusion.1) | data formatting | bytes 6291456 | tf_op jit(solution)/shard_map/transpose | solution.py:129
  11.2 86.5 %shard_map.46 = bf16[2,128,512]{2,1,0:T(8,128)(2,1)} custom-call(bf16[8,384,512]{2,1,0:T(8,128)(2,1)} %bitcast.30, bf16[16,2,96,512]{3,2,1,0:T(8,128)(2,1)} %bitcast.31), custom_call_target="tpu_custom_call" | custom-call | tf_op jit(solution)/shard_map/pallas_call | solution.py:134
  97.8 1.9 %copy.9 = bf16[128,2,512]{2,1,0:T(2,128)(2,1)} copy(bf16[128,2,512]{2,0,1:T(8,128)(2,1)} %bitcast.32) | data formatting | bytes 524288 | tf_op jit(solution)/shard_map/transpose | solution.py:154
Async XLA Ops:
  0.0 1.9 %copy-start = (bf16[2,8,2,96,512]{4,3,2,1,0:T(8,128)(2,1)S(1)}, bf16[2,8,2,96,512]{4,3,2,1,0:T(8,128)(2,1)}, u32[]{:S(2)}) copy-start(bf16[2,8,2,96,512]{4,3,2,1,0:T(8,128)(2,1)} %param.5) | copy-start | bytes 9437188
  7.8 0.9 copy-start.1

commit v2 on v1

--- a/solution.py
+++ b/solution.py
@@ -12,18 +12,32 @@
 
 
 def apply_kernel(
-    n_row, n_col, coef, left, out, held, basis, total, outgoing, partial,
-    send_sem, recv_sem, psend_sem, precv_sem,
+    n_row, n_col, ranks, sources, right, left_in, out, block, bases, left, split, coef, held,
+    basis, total, outgoing, partial,
+    load_sem, send_sem, recv_sem, psend_sem, precv_sem,
 ):
     row, col = lax.axis_index("row"), lax.axis_index("col")
     half = n_row // 2
     side = row // half
     place = row % half
-    depth, samples = coef.shape[1], coef.shape[2]
+    samples = coef.shape[2]
     tiles, _, rank_pad, width = left.shape
     cols = tiles // n_row
     chunks = samples // CHUNK
     share = width // n_col
+    pair = 2 * rank_pad
+    step_rows = 2 * CHUNK
+
+    loads = [
+        pltpu.make_async_copy(
+            sources.at[pl.ds(c * width, width)], block.at[pl.ds(c * width, width)], load_sem.at[c]
+        )
+        for c in range(cols)
+    ]
+    loads.append(pltpu.make_async_copy(right, bases, load_sem.at[cols]))
+    loads.append(pltpu.make_async_copy(left_in, left, load_sem.at[cols + 1]))
+    for load in loads:
+        load.start()
 
     def to_row(k):
         far = k < half
@@ -55,9 +69,45 @@
             device_id_type=MESH,
         )
 
+    at = lax.broadcasted_iota(jnp.int32, (step_rows, step_rows), 0)
+    picked = jnp.where(at < CHUNK, 2 * at, 2 * (at - CHUNK) + 1)
+    unweave = jnp.where(lax.broadcasted_iota(jnp.int32, (step_rows, step_rows), 1) == picked, 1.0, 0.0)
+    unweave = unweave.astype(jnp.bfloat16)
+    levels = lax.broadcasted_iota(jnp.int32, (rank_pad, CHUNK), 0)
+    woven = block.reshape(2 * cols * width, samples)
+
+    def project(dest, lanes):
+        for c in range(cols):
+            prod = jnp.dot(bases[c, dest], split[c], preferred_element_type=jnp.float32)
+            real = prod[:rank_pad, :CHUNK] - prod[rank_pad:, CHUNK:]
+            imag = prod[:rank_pad, CHUNK:] + prod[rank_pad:, :CHUNK]
+            keep = levels < ranks[c, dest]
+            coef[dest, c * pair : c * pair + rank_pad, lanes] = jnp.where(keep, real, 0.0).astype(coef.dtype)
+            coef[dest, c * pair + rank_pad : (c + 1) * pair, lanes] = jnp.where(keep, imag, 0.0).astype(coef.dtype)
+
     for ch in range(chunks):
-        for k in steps:
-            coef_copy(k, to_row(k), row, ch).start()
+        lanes = pl.ds(ch * CHUNK, CHUNK)
+        for c in range(cols):
+            if ch == 0:
+                loads[c].wait()
+            for t in range(width // CHUNK):
+                rows = woven[pl.ds(2 * (c * width + t * CHUNK), step_rows), lanes]
+                apart = jnp.dot(unweave, rows, preferred_element_type=jnp.float32).astype(split.dtype)
+                split[c, t * CHUNK : (t + 1) * CHUNK, :CHUNK] = apart[:CHUNK]
+                split[c, t * CHUNK : (t + 1) * CHUNK, CHUNK:] = apart[CHUNK:]
+        if ch == 0:
+            loads[cols].wait()
+
+        def project_send(k, carry):
+            dest = to_row(k)
+            project(dest, lanes)
+            coef_copy(k, dest, row, ch).start()
+            return carry
+
+        lax.fori_loop(0, half, project_send, 0)
+        lax.fori_loop(half + 1, n_row, project_send, 0)
+        project(row, lanes)
+    loads[cols + 1].wait()
 
     def prepare(a, carry):
         plain, swapped = [], []
@@ -118,15 +168,8 @@
 def body(n_row, n_col, sources_in, right_bases, left_bases, tile_ranks):
     cols, tile_rows, _, rank_pad, width = right_bases.shape
     samples = sources_in.shape[2]
-    blocks = sources_in.reshape(cols, width, 2, samples)
-    prod = jnp.einsum("cmprb,cbqs->cmpqrs", right_bases, blocks, preferred_element_type=jnp.float32)
-    real = prod[:, :, 0, 0] - prod[:, :, 1, 1]
-    imag = prod[:, :, 0, 1] + prod[:, :, 1, 0]
-    levels = lax.broadcasted_iota(jnp.int32, (cols, tile_rows, rank_pad), 2)
-    keep = (levels < tile_ranks.T[:, :, None]).astype(jnp.float32)
-    coeffs = (jnp.stack([real, imag], 2) * keep[:, :, None, :, None]).astype(jnp.bfloat16)
     depth = cols * 2 * rank_pad
-    coeffs = coeffs.transpose(1, 0, 2, 3, 4).reshape(tile_rows, depth, samples)
+    right = right_bases.reshape(cols, tile_rows, 2 * rank_pad, width)
     left = left_bases.reshape(-1, 2, rank_pad, width)
     chunks = samples // CHUNK
     share = width // n_col
@@ -134,14 +177,20 @@
     out = pl.pallas_call(
         functools.partial(apply_kernel, n_row, n_col),
         out_shape=jax.ShapeDtypeStruct((2, share, samples), jnp.bfloat16),
-        in_specs=[vmem, vmem],
+        in_specs=[pl.BlockSpec(memory_space=pltpu.SMEM)] + [pl.BlockSpec(memory_space=pl.ANY)] * 3,
         out_specs=vmem,
         scratch_shapes=[
+            pltpu.VMEM(sources_in.shape, jnp.bfloat16),
+            pltpu.VMEM(right.shape, jnp.bfloat16),
+            pltpu.VMEM(left.shape, jnp.bfloat16),
+            pltpu.VMEM((cols, width, 2 * CHUNK), jnp.bfloat16),
+            pltpu.VMEM((n_row, depth, samples), jnp.bfloat16),
             pltpu.VMEM((n_row, depth, samples), jnp.bfloat16),
             pltpu.VMEM((n_row, 2 * width, depth), jnp.bfloat16),
             pltpu.VMEM((2 * width, CHUNK), jnp.float32),
             pltpu.VMEM((chunks, 2, width, CHUNK), jnp.float32),
             pltpu.VMEM((chunks, n_col - 1, 2, share, CHUNK), jnp.float32),
+            pltpu.SemaphoreType.DMA((cols + 2,)),
             pltpu.SemaphoreType.DMA((n_row, chunks)),
             pltpu.SemaphoreType.DMA((n_row, chunks)),
             pltpu.SemaphoreType.DMA((n_col, chunks)),
@@ -150,7 +199,7 @@
         compiler_params=pltpu.CompilerParams(
             collective_id=0, has_side_effects=True, vmem_limit_bytes=56 * 2**20
         ),
-    )(coeffs, left)
+    )(tile_ranks.T, sources_in, right, left)
     return out.transpose(1, 0, 2)
 
 

time: 99.9 us -> 87.5 us (0.88)
  matrix products: 5 us -> 0 us
  local copies, waits for them, and re-layouts: 5.81 us -> 1.92 us
  other arithmetic: 2.29 us -> 0 us
  Pallas kernels: 86.5 us -> 84.9 us
    dot_general x1 -> x0, matrix products: 5 us -> none  [body(): jnp.einsum('cmprb,cbqs->cmpqrs', right_bases, blocks, preferred_element_t...]
    transpose x1 -> x0, local copies, waits for them, and re-layouts: 1.99 us -> none  [body(): coeffs = coeffs.transpose(1, 0, 2, 3, 4).reshape(tile_rows, depth, samples)]
    unnamed x4 -> x0, local copies, waits for them, and re-layouts: 1.9 us -> none
    pallas_call x1, Pallas kernels: 86.5 us -> 84.9 us  [body(): pl.pallas_call(functools.partial(apply_kernel, n_row, n_col), out_shape=j...]
where the time goes in v2:
time: 87.5 us; the launch traced here: 86.8 us
  Pallas kernels  84.9 us (97%)
  local copies, waits for them, and re-layouts  1.92 us (2%)
    pallas_call x1, Pallas kernels, body(): pl.pallas_call(functools.partial(apply_kernel, n_row, n_col), out_shape=j...  84.9 us
    transpose x1, local copies, waits for them, and re-layouts, body(): return out.transpose(1, 0, 2)  1.92 us

profile of v2, /device:TPU:0, one launch (start us, length us, event | category | flops | bytes accessed | tf_op | source)
XLA Modules:
  0.0 86.8 jit_solution(7452421278968814671)
XLA Ops:
  0.0 84.9 %shard_map.46 = bf16[2,128,512]{2,1,0:T(8,128)(2,1)} custom-call(s32[2,8]{1,0:T(2,128)} %bitcast.7, bf16[1024,2,512]{2,1,0:T(2,128)(2,1)} %sources.1, bf16[2,8,192,512]{3,2,1,0:T(8,128)(2,1)} %bitcast.4, bf16[16,2,96,512]{3,2,1,0:T(8,128)(2,1)} %bitcast.5), custom_call_target="tpu_custom_call" | custom-call | tf_op jit(solution)/shard_map/pallas_call | solution.py:177
  84.9 1.9 %copy.5 = bf16[128,2,512]{2,1,0:T(2,128)(2,1)} copy(bf16[128,2,512]{2,0,1:T(8,128)(2,1)} %bitcast.6) | data formatting | bytes 524288 | tf_op jit(solution)/shard_map/transpose | solution.py:203

commit v3 on v2

--- a/solution.py
+++ b/solution.py
@@ -13,7 +13,7 @@
 
 def apply_kernel(
     n_row, n_col, ranks, sources, right, left_in, out, block, bases, left, split, coef, held,
-    basis, total, outgoing, partial,
+    basis, total, own, outgoing, partial,
     load_sem, send_sem, recv_sem, psend_sem, precv_sem,
 ):
     row, col = lax.axis_index("row"), lax.axis_index("col")
@@ -56,7 +56,6 @@
         pl.semaphore_signal(barrier, inc=1, device_id={"row": (row + k) % n_row}, device_id_type=MESH)
     for k in range(1, n_col):
         pl.semaphore_signal(barrier, inc=1, device_id={"col": (col + k) % n_col}, device_id_type=MESH)
-    pl.semaphore_wait(barrier, n_row + n_col - 2)
 
     def coef_copy(k, dest, slot, ch):
         lanes = pl.ds(ch * CHUNK, CHUNK)
@@ -97,6 +96,7 @@
                 split[c, t * CHUNK : (t + 1) * CHUNK, CHUNK:] = apart[CHUNK:]
         if ch == 0:
             loads[cols].wait()
+            pl.semaphore_wait(barrier, n_row + n_col - 2)
 
         def project_send(k, carry):
             dest = to_row(k)
@@ -132,13 +132,20 @@
             device_id_type=MESH,
         )
 
+    to = lax.broadcasted_iota(jnp.int32, (2 * share, 2 * share), 0)
+    near = lax.broadcasted_iota(jnp.int32, (2 * share, 2 * share), 1)
+    weave = jnp.where(to == jnp.where(near < share, 2 * near, 2 * (near - share) + 1), 1.0, 0.0)
+    weave = weave.astype(jnp.bfloat16)
+    result = out.reshape(2 * share, samples)
+
     def finish(ch):
-        lanes = pl.ds(ch * CHUNK, CHUNK)
-        mine = outgoing[ch, :, pl.ds(pl.multiple_of(col * share, share), share), :]
+        mine = own[ch]
         for k in range(1, n_col):
             partial_copy(k, ch).wait_recv()
-            mine = mine + partial[ch, k - 1]
-        out[:, :, lanes] = mine.astype(out.dtype)
+            mine = mine + partial[ch, k - 1].astype(jnp.float32)
+        rounded = mine.astype(out.dtype).reshape(2 * share, CHUNK)
+        woven_out = jnp.dot(weave, rounded, preferred_element_type=jnp.float32)
+        result[:, pl.ds(ch * CHUNK, CHUNK)] = woven_out.astype(out.dtype)
 
     for ch in range(chunks):
         lanes = pl.ds(ch * CHUNK, CHUNK)
@@ -152,7 +159,9 @@
 
         lax.fori_loop(half + 1, n_row, take, 0)
         lax.fori_loop(0, half, take, 0)
-        outgoing[ch] = total[...].reshape(2, width, CHUNK)
+        outgoing[ch] = total[...].reshape(2, width, CHUNK).astype(outgoing.dtype)
+        for q in range(2):
+            own[ch, q] = total[pl.ds(pl.multiple_of(q * width + col * share, share), share)]
         for k in range(1, n_col):
             partial_copy(k, ch).start()
         if ch > 0:
@@ -174,9 +183,9 @@
     chunks = samples // CHUNK
     share = width // n_col
     vmem = pl.BlockSpec(memory_space=pltpu.VMEM)
-    out = pl.pallas_call(
+    return pl.pallas_call(
         functools.partial(apply_kernel, n_row, n_col),
-        out_shape=jax.ShapeDtypeStruct((2, share, samples), jnp.bfloat16),
+        out_shape=jax.ShapeDtypeStruct((share, 2, samples), jnp.bfloat16),
         in_specs=[pl.BlockSpec(memory_space=pltpu.SMEM)] + [pl.BlockSpec(memory_space=pl.ANY)] * 3,
         out_specs=vmem,
         scratch_shapes=[
@@ -188,8 +197,9 @@
             pltpu.VMEM((n_row, depth, samples), jnp.bfloat16),
             pltpu.VMEM((n_row, 2 * width, depth), jnp.bfloat16),
             pltpu.VMEM((2 * width, CHUNK), jnp.float32),
-            pltpu.VMEM((chunks, 2, width, CHUNK), jnp.float32),
-            pltpu.VMEM((chunks, n_col - 1, 2, share, CHUNK), jnp.float32),
+            pltpu.VMEM((chunks, 2, share, CHUNK), jnp.float32),
+            pltpu.VMEM((chunks, 2, width, CHUNK), jnp.bfloat16),
+            pltpu.VMEM((chunks, n_col - 1, 2, share, CHUNK), jnp.bfloat16),
             pltpu.SemaphoreType.DMA((cols + 2,)),
             pltpu.SemaphoreType.DMA((n_row, chunks)),
             pltpu.SemaphoreType.DMA((n_row, chunks)),
@@ -200,7 +210,6 @@
             collective_id=0, has_side_effects=True, vmem_limit_bytes=56 * 2**20
         ),
     )(tile_ranks.T, sources_in, right, left)
-    return out.transpose(1, 0, 2)
 
 
 def solution(mesh):

time: 87.5 us -> 84.8 us (0.969)
  Pallas kernels: 84.9 us -> 82.7 us
    pallas_call x1, Pallas kernels: 84.9 us -> 82.7 us  [body(): pl.pallas_call(functools.partial(apply_kernel, n_row, n_col), out_shape=j...]
    transpose x1 -> x0, local copies, waits for them, and re-layouts: 1.92 us -> none  [body(): return out.transpose(1, 0, 2)]
    unnamed x0 -> x1, local copies, waits for them, and re-layouts: none -> 1.83 us
where the time goes in v3:
time: 84.8 us; the launch traced here: 84.5 us
  Pallas kernels  82.7 us (98%)
  local copies, waits for them, and re-layouts  1.83 us (2%)
    pallas_call x1, Pallas kernels, body(): pl.pallas_call(functools.partial(apply_kernel, n_row, n_col), out_shape=j...  82.7 us
    unnamed x1, local copies, waits for them, and re-layouts  1.83 us

profile of v3, /device:TPU:0, one launch (start us, length us, event | category | flops | bytes accessed | tf_op | source)
XLA Modules:
  0.0 84.5 jit_solution(335005126167612907)
XLA Ops:
  0.0 82.7 %shard_map.46 = bf16[128,2,512]{2,1,0:T(2,128)(2,1)} custom-call(s32[2,8]{1,0:T(2,128)} %bitcast.5, bf16[1024,2,512]{2,1,0:T(2,128)(2,1)} %sources.1, bf16[2,8,192,512]{3,2,1,0:T(8,128)(2,1)} %bitcast.3, bf16[16,2,96,512]{3,2,1,0:T(8,128)(2,1)} %bitcast.4), custom_call_target="tpu_custom_call" | custom-call | tf_op jit(solution)/shard_map/pallas_call | solution.py:186
  82.7 1.8 %copy.6 = bf16[128,2,512]{2,1,0:T(2,128)(2,1)} copy(bf16[128,2,512]{2,1,0:T(2,128)(2,1)} %shard_map.46) | data formatting | bytes 524288

commit v4 on v3

--- a/solution.py
+++ b/solution.py
@@ -28,16 +28,18 @@
     pair = 2 * rank_pad
     step_rows = 2 * CHUNK
 
-    loads = [
-        pltpu.make_async_copy(
-            sources.at[pl.ds(c * width, width)], block.at[pl.ds(c * width, width)], load_sem.at[c]
-        )
-        for c in range(cols)
-    ]
-    loads.append(pltpu.make_async_copy(right, bases, load_sem.at[cols]))
-    loads.append(pltpu.make_async_copy(left_in, left, load_sem.at[cols + 1]))
-    for load in loads:
-        load.start()
+    def load_part(ch):
+        lanes = pl.ds(ch * CHUNK, CHUNK)
+        return pltpu.make_async_copy(sources.at[:, :, lanes], block.at[:, :, lanes], load_sem.at[ch])
+
+    def load_bases(there, at):
+        span = pl.ds(there * half, half)
+        return pltpu.make_async_copy(right.at[:, span], bases.at[:, span], load_sem.at[chunks + at])
+
+    far_bases, near_bases = load_bases(1 - side, 0), load_bases(side, 1)
+    load_left = pltpu.make_async_copy(left_in, left, load_sem.at[chunks + 2])
+    load_part(0).start()
+    far_bases.start()
 
     def to_row(k):
         far = k < half
@@ -87,15 +89,19 @@
     for ch in range(chunks):
         lanes = pl.ds(ch * CHUNK, CHUNK)
         for c in range(cols):
-            if ch == 0:
-                loads[c].wait()
+            if c == 0:
+                load_part(ch).wait()
             for t in range(width // CHUNK):
                 rows = woven[pl.ds(2 * (c * width + t * CHUNK), step_rows), lanes]
                 apart = jnp.dot(unweave, rows, preferred_element_type=jnp.float32).astype(split.dtype)
                 split[c, t * CHUNK : (t + 1) * CHUNK, :CHUNK] = apart[:CHUNK]
                 split[c, t * CHUNK : (t + 1) * CHUNK, CHUNK:] = apart[CHUNK:]
         if ch == 0:
-            loads[cols].wait()
+            far_bases.wait()
+            near_bases.start()
+            for later in range(1, chunks):
+                load_part(later).start()
+            load_left.start()
             pl.semaphore_wait(barrier, n_row + n_col - 2)
 
         def project_send(k, carry):
@@ -105,9 +111,11 @@
             return carry
 
         lax.fori_loop(0, half, project_send, 0)
+        if ch == 0:
+            near_bases.wait()
         lax.fori_loop(half + 1, n_row, project_send, 0)
         project(row, lanes)
-    loads[cols + 1].wait()
+    load_left.wait()
 
     def prepare(a, carry):
         plain, swapped = [], []
@@ -200,7 +208,7 @@
             pltpu.VMEM((chunks, 2, share, CHUNK), jnp.float32),
             pltpu.VMEM((chunks, 2, width, CHUNK), jnp.bfloat16),
             pltpu.VMEM((chunks, n_col - 1, 2, share, CHUNK), jnp.bfloat16),
-            pltpu.SemaphoreType.DMA((cols + 2,)),
+            pltpu.SemaphoreType.DMA((chunks + 3,)),
             pltpu.SemaphoreType.DMA((n_row, chunks)),
             pltpu.SemaphoreType.DMA((n_row, chunks)),
             pltpu.SemaphoreType.DMA((n_col, chunks)),

time: 84.8 us -> 84.1 us (level)
  no operation moved by 1% of the time
where the time goes in v4:
time: 84.1 us; the launch traced here: 83.9 us
  Pallas kernels  82 us (98%)
  local copies, waits for them, and re-layouts  1.83 us (2%)
    pallas_call x1, Pallas kernels, body(): pl.pallas_call(functools.partial(apply_kernel, n_row, n_col), out_shape=j...  82 us
    unnamed x1, local copies, waits for them, and re-layouts  1.83 us

profile of v4, /device:TPU:0, one launch (start us, length us, event | category | flops | bytes accessed | tf_op | source)
XLA Modules:
  0.0 83.9 jit_solution(8038494854709822233)
XLA Ops:
  0.0 82.0 %shard_map.46 = bf16[128,2,512]{2,1,0:T(2,128)(2,1)} custom-call(s32[2,8]{1,0:T(2,128)} %bitcast.5, bf16[1024,2,512]{2,1,0:T(2,128)(2,1)} %sources.1, bf16[2,8,192,512]{3,2,1,0:T(8,128)(2,1)} %bitcast.3, bf16[16,2,96,512]{3,2,1,0:T(8,128)(2,1)} %bitcast.4), custom_call_target="tpu_custom_call" | custom-call | tf_op jit(solution)/shard_map/pallas_call | solution.py:194
  82.0 1.8 %copy.6 = bf16[128,2,512]{2,1,0:T(2,128)(2,1)} copy(bf16[128,2,512]{2,1,0:T(2,128)(2,1)} %shard_map.46) | data formatting | bytes 524288

commit v5 on v4

--- a/solution.py
+++ b/solution.py
@@ -191,33 +191,36 @@
     chunks = samples // CHUNK
     share = width // n_col
     vmem = pl.BlockSpec(memory_space=pltpu.VMEM)
+    scratch = [
+        pltpu.VMEM(sources_in.shape, jnp.bfloat16),
+        pltpu.VMEM(right.shape, jnp.bfloat16),
+        pltpu.VMEM(left.shape, jnp.bfloat16),
+        pltpu.VMEM((cols, width, 2 * CHUNK), jnp.bfloat16),
+        pltpu.VMEM((n_row, depth, samples), jnp.bfloat16),
+        pltpu.VMEM((n_row, depth, samples), jnp.bfloat16),
+        pltpu.VMEM((n_row, 2 * width, depth), jnp.bfloat16),
+        pltpu.VMEM((2 * width, CHUNK), jnp.float32),
+        pltpu.VMEM((chunks, 2, share, CHUNK), jnp.float32),
+        pltpu.VMEM((chunks, 2, width, CHUNK), jnp.bfloat16),
+        pltpu.VMEM((chunks, n_col - 1, 2, share, CHUNK), jnp.bfloat16),
+        pltpu.SemaphoreType.DMA((chunks + 3,)),
+        pltpu.SemaphoreType.DMA((n_row, chunks)),
+        pltpu.SemaphoreType.DMA((n_row, chunks)),
+        pltpu.SemaphoreType.DMA((n_col, chunks)),
+        pltpu.SemaphoreType.DMA((n_col, chunks)),
+    ]
+    held_bytes = sum(x.size * x.dtype.itemsize for x in (sources_in, right, left))
+    held_bytes += n_row * depth * (2 * samples + 2 * width) * 2
     return pl.pallas_call(
         functools.partial(apply_kernel, n_row, n_col),
         out_shape=jax.ShapeDtypeStruct((share, 2, samples), jnp.bfloat16),
-        in_specs=[pl.BlockSpec(memory_space=pltpu.SMEM)] + [pl.BlockSpec(memory_space=pl.ANY)] * 3,
+        in_specs=[pl.BlockSpec(memory_space=pltpu.SMEM)] + [pl.BlockSpec(memory_space=pltpu.HBM)] * 3,
         out_specs=vmem,
-        scratch_shapes=[
-            pltpu.VMEM(sources_in.shape, jnp.bfloat16),
-            pltpu.VMEM(right.shape, jnp.bfloat16),
-            pltpu.VMEM(left.shape, jnp.bfloat16),
-            pltpu.VMEM((cols, width, 2 * CHUNK), jnp.bfloat16),
-            pltpu.VMEM((n_row, depth, samples), jnp.bfloat16),
-            pltpu.VMEM((n_row, depth, samples), jnp.bfloat16),
-            pltpu.VMEM((n_row, 2 * width, depth), jnp.bfloat16),
-            pltpu.VMEM((2 * width, CHUNK), jnp.float32),
-            pltpu.VMEM((chunks, 2, share, CHUNK), jnp.float32),
-            pltpu.VMEM((chunks, 2, width, CHUNK), jnp.bfloat16),
-            pltpu.VMEM((chunks, n_col - 1, 2, share, CHUNK), jnp.bfloat16),
-            pltpu.SemaphoreType.DMA((chunks + 3,)),
-            pltpu.SemaphoreType.DMA((n_row, chunks)),
-            pltpu.SemaphoreType.DMA((n_row, chunks)),
-            pltpu.SemaphoreType.DMA((n_col, chunks)),
-            pltpu.SemaphoreType.DMA((n_col, chunks)),
-        ],
+        scratch_shapes=scratch,
         compiler_params=pltpu.CompilerParams(
-            collective_id=0, has_side_effects=True, vmem_limit_bytes=56 * 2**20
+            collective_id=0, has_side_effects=True, vmem_limit_bytes=held_bytes + 12 * 2**20
         ),
-    )(tile_ranks.T, sources_in, right, left)
+    )(tile_ranks.T, *[pltpu.with_memory_space_constraint(x, pltpu.HBM) for x in (sources_in, right, left)])
 
 
 def solution(mesh):

time: 84.1 us -> 82.8 us (0.985)
    unnamed x1 -> x3, local copies, waits for them, and re-layouts: 1.83 us -> 1.38 us
where the time goes in v5:
time: 82.8 us; the launch traced here: 82.6 us
  Pallas kernels  81.2 us (98%)
  local copies, waits for them, and re-layouts  1.38 us (2%)
    pallas_call x1, Pallas kernels, body(): pl.pallas_call(functools.partial(apply_kernel, n_row, n_col), out_shape=j...  81.2 us

profile of v5, /device:TPU:0, one launch (start us, length us, event | category | flops | bytes accessed | tf_op | source)
XLA Modules:
  0.0 82.6 jit_solution(9446147904645071817)
XLA Ops:
  0.0 0.0 copy-start
  0.0 0.7 copy-done
  0.7 81.2 %shard_map.46 = bf16[128,2,512]{2,1,0:T(2,128)(2,1)S(1)} custom-call(s32[2,8]{1,0:T(2,128)S(1)} %bitcast.3, bf16[1024,2,512]{2,1,0:T(2,128)(2,1)} %sources.1, bf16[2,8,192,512]{3,2,1,0:T(8,128)(2,1)} %bitcast.4, bf16[16,2,96,512]{3,2,1,0:T(8,128)(2,1)} %bitcast.5), custom_call_target="tpu_custom_call" | custom-call | tf_op jit(solution)/shard_map/pallas_call | solution.py:214
  81.9 0.7 copy.6
Async XLA Ops:
  0.0 0.7 copy-start
